TPU v7x, 512 devices: a whole 4x4x16 slice. The times are simulated.
512 devices in a mesh: section: 8 (over y_lo, x), fsdp: 64 (over y_hi, z, core).
Axes of the slice: x: 4, y: 4 (y_hi: 2, y_lo: 2; y = y_hi * 2 + y_lo), z: 16, core: 2. Of those that a mesh axis runs over, the one named last changes fastest.
Arguments:
- inputs: bfloat16 [8, 8, 128, 64, 256], P('section', None, 'fsdp'), may hold values from -6 to 6
- conv_first: bfloat16 [8, 27, 256, 256], P('section', None, 'fsdp'), may hold values from -0.078125 to 0.078125
- conv_second: bfloat16 [8, 27, 256, 256], P('section', None, 'fsdp'), may hold values from -0.078125 to 0.078125
- gain_first: float32 [8, 256], P('section'), may hold values from 0.5 to 2
- gain_second: float32 [8, 256], P('section'), may hold values from 0.5 to 2
- skip_weight: bfloat16 [4, 256, 256], P(None, 'fsdp'), may hold values from -0.375 to 0.375
Outputs:
- section_out: bfloat16 [8, 8, 128, 64, 256], P('section', None, 'fsdp')
All inputs are finite; a program needn't handle non-finite values.
Results may differ from a plain program's by a relative error of at most 0.008.
Values may be sent and summed in bfloat16 or wider, within the bound.
A program may use at most 64 MiB of HBM per device.

v0:
```python
import jax
import jax.numpy as jnp
from jax import lax
from jax.sharding import PartitionSpec as P


def extended(cells, sides, width):
    for axis, dim in sides:
        count = lax.axis_size(axis)
        ends = count - 1
        head = lax.slice_in_dim(cells, 0, width, axis=dim)
        tail = lax.slice_in_dim(cells, cells.shape[dim] - width, cells.shape[dim], axis=dim)
        cells = jnp.concatenate(
            [
                lax.ppermute(tail, axis, [(i, (i + 1) % count) for i in range(ends)]),
                cells,
                lax.ppermute(head, axis, [((i + 1) % count, i) for i in range(ends)]),
            ],
            axis=dim,
        )
    return cells


def activated(values, gain_row):
    wide_values = values.astype(jnp.float32)
    scale = lax.rsqrt(jnp.mean(wide_values * wide_values, axis=-1, keepdims=True) + 1e-06)
    return jax.nn.silu(wide_values * scale * gain_row)


def padded_rim(values):
    grown = extended(values, (("fsdp", 1),), 1)
    return jnp.pad(grown, ((1, 1), (0, 0), (1, 1), (0, 0)))


def tap_sum(padded, kernel, cells, channels):
    depth_n = padded.shape[0] - 2
    rows_n = padded.shape[1] - 2
    wide_n = padded.shape[2] - 2
    running = jnp.zeros((cells, channels), jnp.float32)
    for tap_index in range(27):
        off_depth, remainder = divmod(tap_index, 9)
        off_rows, off_wide = divmod(remainder, 3)
        window = padded[
            off_depth : off_depth + depth_n,
            off_rows : off_rows + rows_n,
            off_wide : off_wide + wide_n,
        ]
        running = running + jnp.dot(
            window.reshape(-1, padded.shape[3]),
            kernel[tap_index],
            preferred_element_type=jnp.float32,
        )
    return running


def shards(inputs, conv_first, conv_second, gain_first, gain_second, skip_weight):
    section_id = lax.axis_index("section")
    section_count = lax.axis_size("section")
    half_count = section_count // 2
    current = inputs[0]
    map_shape = current.shape
    channels = map_shape[3]
    cells = map_shape[0] * map_shape[1] * map_shape[2]
    kernel_one = conv_first[0]
    kernel_two = conv_second[0]
    first = activated(current, gain_first[0]).astype(jnp.bfloat16)

    def layer_kernel(kernel_shard):
        return lax.all_gather(kernel_shard, "fsdp", axis=1, tiled=True)

    hidden = tap_sum(padded_rim(first), layer_kernel(kernel_one), cells, channels)
    second = activated(hidden.reshape(map_shape), gain_second[0]).astype(jnp.bfloat16)
    branch_out = tap_sum(padded_rim(second), layer_kernel(kernel_two), cells, channels)
    block = (current.astype(jnp.float32) + branch_out.reshape(map_shape)).astype(jnp.bfloat16)
    decoder_pos = jnp.clip(section_id - half_count, 0, half_count - 1)
    local_rows = lax.dynamic_index_in_dim(skip_weight, decoder_pos, 0, keepdims=False)
    full_skip = lax.all_gather(local_rows, "fsdp", axis=0, tiled=True)
    every_block = lax.all_gather(block[None], "section", axis=0, tiled=True)
    paired = lax.dynamic_index_in_dim(every_block, decoder_pos, 0, keepdims=False)
    projection = jnp.dot(
        paired.reshape(-1, channels), full_skip, preferred_element_type=jnp.float32
    )
    joined = (block.astype(jnp.float32) + projection.reshape(map_shape)).astype(jnp.bfloat16)
    result_map = jnp.where(section_id >= half_count, joined, block)
    return result_map[None]


def solution(mesh):
    in_specs = (
        P("section", None, "fsdp", None, None),
        P("section", None, "fsdp", None),
        P("section", None, "fsdp", None),
        P("section", None),
        P("section", None),
        P(None, "fsdp", None),
    )
    out_specs = P("section", None, "fsdp", None, None)
    return jax.shard_map(shards, mesh=mesh, in_specs=in_specs, out_specs=out_specs, check_vma=False)
```

profile of v0, /device:TPU:24, one launch (start us, length us, event | category | flops | bytes accessed | tf_op | source)
XLA Modules:
  0.0 425.9 jit_solution(15609588614017645639)
XLA Ops:
  6.5 1.5 copy.10
  8.1 1.3 fusion.65
  9.4 1.4 fusion.72
  10.9 1.9 collective-permute-start
  12.8 11.5 %collective-permute-start.1 = (bf16[8,1,64,256]{3,2,1,0:T(8,128)(2,1)S(1)}, bf16[8,1,64,256]{3,2,1,0:T(8,128)(2,1)S(1)}, u32[]{:S(2)}, u32[]{:S(2)}) collective-permute-start(bf16[8,1,64,256]{3,2,1,0:T(8,128)(2,1)S(1)} %get-tuple-element.114), channel_id=1, source_target_pairs={{1,0},{2,1},{3,2},{4,3},{5,4},{6,5},{7,6},{8,7},{9,8},{10,9},{11,1... | collective-permute-start | bytes 786440 | tf_op jit(solution)/shard_map/ppermute | solution.py:17
  24.3 1.4 copy.38
  25.9 1.2 fusion.80
  27.1 1.1 collective-permute-done.1
  28.2 0.6 fusion.13
  28.9 4.3 %fusion.144 = (bf16[8,2,64,256]{3,2,1,0:T(8,128)(2,1)S(1)}, bf16[8,2,64,256]{3,2,1,0:T(8,128)(2,1)}, bf16[8,2,64,256]{3,2,1,0:T(8,128)(2,1)}, bf16[8,2,64,256]{3...) fusion(bf16[10,4,66,256]{3,2,1,0:T(8,128)(2,1)S(1)} %fusion.13), kind=kLoop, calls=%fused_computation.222 | loop fusion | bytes 19922944 | tf_op jit(solution)/shard_map/slice | solution.py:43
  33.2 1.9 fusion.145
  35.1 1.1 pad_maximum_fusion.3
  36.2 128.2 %all-gather.9.cloned.1.call-done = bf16[1,27,256,256]{3,1,0,2:T(8,128)(2,1)} async-done(((bf16[1,27,4,256]{3,1,0,2:T(8,128)(2,1)}), bf16[1,27,256,256]{3,1,0,2:T(8,128)(2,1)}) %all-gather.9.cloned.1.call-update) | async-done | bytes 3538960 | tf_op jit(solution)/shard_map/all_gather | solution.py:69
  164.4 10.8 %fusion.140 = (bf16[1,1,256,256]{3,1,0,2:T(2,128)(2,1)S(1)}, bf16[1,1,256,256]{3,1,0,2:T(2,128)(2,1)S(1)}, bf16[1,1,256,256]{3,1,0,2:T(2,128)(2,1)S(1)}, bf16[1,...) fusion(bf16[1,27,256,256]{3,1,0,2:T(8,128)(2,1)} %all-gather.9., ...), kind=kLoop, calls=%fused_computation.218 | loop fusion | bytes 4980736 | tf_op jit(solution)/shard_map/slice | solution.py:50
  175.9 0.4 copy-done.20
  177.2 1.0 copy-done.3
  178.2 1.9 fusion.141
  180.1 0.3 fusion.129
  184.7 0.3 fusion.116
  186.0 0.3 fusion.121
  187.1 0.8 fusion.58
  187.9 0.9 multiply_reduce_fusion
  188.9 0.4 multiply_convert_fusion.1
  189.3 2.1 collective-permute-start.2
  191.5 7.0 %collective-permute-start.3 = (bf16[8,1,64,256]{3,2,1,0:T(8,128)(2,1)S(1)}, bf16[8,1,64,256]{3,2,1,0:T(8,128)(2,1)S(1)}, u32[]{:S(2)}, u32[]{:S(2)}) collective-permute-start(bf16[8,1,64,256]{3,2,1,0:T(8,128)(2,1)S(1)} %get-tuple-element.110), channel_id=1, source_target_pairs={{1,0},{2,1},{3,2},{4,3},{5,4},{6,5},{7,6},{8,7},{9,8},{10,9},{11,1... | collective-permute-start | bytes 786440 | tf_op jit(solution)/shard_map/ppermute | solution.py:17
  198.5 114.6 %all-gather.11.cloned.1.call-done = bf16[1,27,256,256]{3,1,0,2:T(8,128)(2,1)} async-done(((bf16[1,27,4,256]{3,1,0,2:T(8,128)(2,1)}), bf16[1,27,256,256]{3,1,0,2:T(8,128)(2,1)}) %all-gather.11.cloned.1.call-update) | async-done | bytes 3538960 | tf_op jit(solution)/shard_map/all_gather | solution.py:69
  313.1 11.0 %fusion.138 = (bf16[1,1,256,256]{3,1,0,2:T(2,128)(2,1)S(1)}, bf16[1,1,256,256]{3,1,0,2:T(2,128)(2,1)S(1)}, bf16[1,1,256,256]{3,1,0,2:T(2,128)(2,1)S(1)}, bf16[1,...) fusion(bf16[1,27,256,256]{3,1,0,2:T(8,128)(2,1)} %all-gather.11, ...), kind=kLoop, calls=%fused_computation.216 | loop fusion | bytes 4980736 | tf_op jit(solution)/shard_map/slice | solution.py:50
  324.2 1.7 fusion.139
  325.9 0.5 fusion.84
  326.4 0.7 select_maximum_fusion
  327.1 3.0 fusion.142
  330.1 0.6 fusion.143
  332.1 0.3 fusion.98
  332.4 0.3 fusion.99
  333.0 0.3 fusion.105
  333.3 0.3 fusion.106
  334.2 0.3 fusion.109
  335.1 0.3 fusion.88
  335.4 0.3 fusion.89
  336.0 0.3 fusion.91
  336.3 0.3 fusion.92
  336.9 0.3 fusion.94
  337.2 0.3 fusion.95
  338.1 1.0 fusion.60
  339.1 0.8 fusion.61
  339.9 1.0 fusion.81
  340.9 76.4 %all-gather.2 = bf16[1,256,256]{2,0,1:T(2,128)(2,1)S(1)} all-gather(bf16[1,4,256]{2,0,1:T(2,128)(2,1)S(1)} %copy.69), channel_id=4, replica_groups=mesh['section'=8,'fsdp'=64] {'fsdp'}, dimensions={1}, use_global_device_ids=true | all-gather | bytes 133120 | tf_op jit(solution)/shard_map/all_gather | solution.py:77
  417.3 2.2 fusion.64
  (113 shorter events, 11.8 us)
Async XLA Ops:
  6.5 334.3 %copy-start = (bf16[4,4,256]{2,1,0:T(4,128)(2,1)S(1)}, bf16[4,4,256]{2,1,0:T(4,128)(2,1)}, u32[]{:S(2)}) copy-start(bf16[4,4,256]{2,1,0:T(4,128)(2,1)} %param.11) | copy-start | bytes 24580
  6.5 19.3 %copy-start.1 = (bf16[1,8,2,64,256]{4,3,2,1,0:T(8,128)(2,1)S(1)}, bf16[1,8,2,64,256]{4,3,2,1,0:T(8,128)(2,1)}, u32[]{:S(2)}) copy-start(bf16[1,8,2,64,256]{4,3,2,1,0:T(8,128)(2,1)} %param.6) | copy-start | bytes 1572868
  6.5 19.3 %copy-start.29 = (f32[1,256]{1,0:T(1,128)S(1)}, f32[1,256]{1,0:T(1,128)}, u32[]{:S(2)}) copy-start(f32[1,256]{1,0:T(1,128)} %param.9) | copy-start | bytes 3076
  6.5 157.8 %all-gather.9.cloned.1.call-start = ((), (), s32[]{:S(2)}) async-start(), calls=%async_computation.1 | async-start | bytes 4259840 | tf_op jit(solution)/shard_map/all_gather | solution.py:69
  8.1 305.1 %all-gather.11.cloned.1.call-start = ((), (), s32[]{:S(2)}) async-start(), calls=%async_computation.2 | async-start | bytes 4259840 | tf_op jit(solution)/shard_map/all_gather | solution.py:69
  10.9 16.2 %collective-permute-start = (bf16[8,1,64,256]{3,2,1,0:T(8,128)(2,1)S(1)}, bf16[8,1,64,256]{3,2,1,0:T(8,128)(2,1)S(1)}, u32[]{:S(2)}, u32[]{:S(2)}) collective-permute-start(bf16[8,1,64,256]{3,2,1,0:T(8,128)(2,1)S(1)} %get-tuple-element.113), channel_id=1, source_target_pairs={{0,1},{1,2},{2,3},{3,4},{4,5},{5,6},{6,7},{7,8},{8,9},{9,10},{10,1... | collective-permute-start | bytes 786440 | tf_op jit(solution)/shard_map/ppermute | solution.py:15
  12.8 15.4 %collective-permute-start.1 = (bf16[8,1,64,256]{3,2,1,0:T(8,128)(2,1)S(1)}, bf16[8,1,64,256]{3,2,1,0:T(8,128)(2,1)S(1)}, u32[]{:S(2)}, u32[]{:S(2)}) collective-permute-start(bf16[8,1,64,256]{3,2,1,0:T(8,128)(2,1)S(1)} %get-tuple-element.114), channel_id=1, source_target_pairs={{1,0},{2,1},{3,2},{4,3},{5,4},{6,5},{7,6},{8,7},{9,8},{10,9},{11,1... | collective-permute-start | bytes 786440 | tf_op jit(solution)/shard_map/ppermute | solution.py:17
  25.8 391.5 %all-gather.7.cloned.1.call-start = ((), (), s32[]{:S(2)}) async-start(), calls=%async_computation | async-start | bytes 4718592 | tf_op jit(solution)/shard_map/all_gather | solution.py:78
  28.2 0.7 copy-start.27
  33.2 1.9 copy-start.28
  36.2 139.4 %copy-start.21 = (bf16[8,2,64,256]{3,2,1,0:T(8,128)(2,1)S(1)}, bf16[8,2,64,256]{3,2,1,0:T(8,128)(2,1)}, u32[]{:S(2)}) copy-start(bf16[8,2,64,256]{3,2,1,0:T(8,128)(2,1)} %get-tuple-element.95) | copy-start | bytes 1572868
  164.4 10.9 %copy-start.22 = (bf16[8,2,64,256]{3,2,1,0:T(8,128)(2,1)S(1)}, bf16[8,2,64,256]{3,2,1,0:T(8,128)(2,1)}, u32[]{:S(2)}) copy-start(bf16[8,2,64,256]{3,2,1,0:T(8,128)(2,1)} %get-tuple-element.94) | copy-start | bytes 1572868
  175.2 1.0 copy-start.20
  175.2 1.3 copy-start.19
  175.5 1.3 copy-start.18
  175.9 2.3 copy-start.3
  176.9 3.2 copy-start.15
  178.2 2.2 copy-start.13
  178.2 2.6 copy-start.12
  180.1 1.0 copy-start.25
  180.4 1.1 copy-start.17
  180.7 1.1 copy-start.16
  181.0 1.1 copy-start.14
  181.4 1.1 copy-start.23
  181.8 1.1 copy-start.11
  182.1 1.1 copy-start.10
  182.5 1.1 copy-start.9
  182.9 1.1 copy-start.8
  183.2 1.1 copy-start.7
  183.6 1.1 copy-start.6
  183.9 1.1 copy-start.5
  184.3 1.1 copy-start.4
  185.4 1.1 copy-start.24
  186.0 1.1 copy-start.26
  187.9 1.0 copy-start.30
  189.3 137.1 %collective-permute-start.2 = (bf16[8,1,64,256]{3,2,1,0:T(8,128)(2,1)S(1)}, bf16[8,1,64,256]{3,2,1,0:T(8,128)(2,1)S(1)}, u32[]{:S(2)}, u32[]{:S(2)}) collective-permute-start(bf16[8,1,64,256]{3,2,1,0:T(8,128)(2,1)S(1)} %get-tuple-element.109), channel_id=1, source_target_pairs={{0,1},{1,2},{2,3},{3,4},{4,5},{5,6},{6,7},{7,8},{8,9},{9,10},{10,1... | collective-permute-start | bytes 786440 | tf_op jit(solution)/shard_map/ppermute | solution.py:15
  191.5 134.9 %collective-permute-start.3 = (bf16[8,1,64,256]{3,2,1,0:T(8,128)(2,1)S(1)}, bf16[8,1,64,256]{3,2,1,0:T(8,128)(2,1)S(1)}, u32[]{:S(2)}, u32[]{:S(2)}) collective-permute-start(bf16[8,1,64,256]{3,2,1,0:T(8,128)(2,1)S(1)} %get-tuple-element.110), channel_id=1, source_target_pairs={{1,0},{2,1},{3,2},{4,3},{5,4},{6,5},{7,6},{8,7},{9,8},{10,9},{11,1... | collective-permute-start | bytes 786440 | tf_op jit(solution)/shard_map/ppermute | solution.py:17
  313.1 11.0 %copy-start.2 = (bf16[1,27,256,256]{3,1,0,2:T(8,128)(2,1)S(1)}, bf16[1,27,256,256]{3,1,0,2:T(8,128)(2,1)}, u32[]{:S(2)}) copy-start(bf16[1,27,256,256]{3,1,0,2:T(8,128)(2,1)} %all-gather.11.cloned.1.call-done) | copy-start | bytes 10616836
Sparse Core Ops, SparseCore 0:
  10.7 153.6 all-gather.8
  167.6 145.4 all-gather.10
  341.0 56.4 all-gather.6
where the time goes:
time: 428 us; the launch traced here: 426 us
  waiting for transfers between devices  244 us (57%)
  blocking collectives  76.4 us (18%)
  local copies, waits for them, and re-layouts  40.9 us (10%)
  starting transfers between devices  22.7 us (5%)
  matrix products  20.6 us (5%)
  between operations  13.7 us (3%)
  other arithmetic  7.7 us (2%)
    all_gather x2, waiting for transfers between devices, layer_kernel(): return lax.all_gather(kernel_shard, 'fsdp', axis=1, tiled=True)  243 us
    all_gather x1, blocking collectives, shards(): full_skip = lax.all_gather(local_rows, 'fsdp', axis=0, tiled=True)  76.4 us
    slice x4, local copies, waits for them, and re-layouts, tap_sum(): kernel[tap_index]  25.5 us
    ppermute x2, starting transfers between devices, extended(): lax.ppermute(head, axis, [((i + 1) % count, i) for i in range(ends)])  18.5 us
    dot_general x54, matrix products, tap_sum(): jnp.dot(window.reshape(-1, padded.shape[3]), kernel[tap_index], preferred...  18.5 us
    slice x4, local copies, waits for them, and re-layouts, tap_sum(): padded[off_depth:off_depth + depth_n, off_rows:off_rows + rows_n, off_wid...  9.86 us
  transfers between devices with their start and end apart: 7, of which 3 were waited for; matrix products, arithmetic and copies ran while one was open for 11% of the time, Pallas kernels for 0%

commit v1 on v0

v1 whole, which is shorter than its diff:
```python
import functools

import jax
import jax.numpy as jnp
import numpy as np
from jax import lax
from jax.experimental import pallas as pl
from jax.experimental.pallas import tpu as pltpu
from jax.sharding import PartitionSpec as P

MESH = pl.DeviceIdType.MESH
NZ = 16
RIGHT_STEPS = 8
LEFT_STEPS = 7
MIB = 1 << 20


def gather_kernel(ws_ref, g_ref, local_sem, pair_send, pair_recv, ring_send, ring_recv, core_send, core_recv):
    section = lax.axis_index("section")
    me = lax.axis_index("fsdp")
    h, z, c = me // 32, (me // 2) % NZ, me % 2

    def device(h_at, z_at, c_at):
        return (section, h_at * 32 + z_at * 2 + c_at)

    partner = device(1 - h, z, c)
    sibling = device(h, z, 1 - c)
    neighbours = (device(h, (z + 1) % NZ, c), device(h, (z + NZ - 1) % NZ, c))

    barrier = pltpu.get_barrier_semaphore()
    for other in (partner, sibling) + neighbours:
        pl.semaphore_signal(barrier, inc=1, device_id=other, device_id_type=MESH)
    pl.semaphore_wait(barrier, 4)

    def half(q):
        return h if q == 0 else 1 - h

    def origin(direction, step):
        return (z + NZ - step) % NZ if direction == 0 else (z + step) % NZ

    def remote(src, slot, to, send, recv):
        return pltpu.make_async_remote_copy(
            src_ref=src, dst_ref=slot, send_sem=send, recv_sem=recv, device_id=to, device_id_type=MESH
        )

    def pair_copy(k):
        return remote(ws_ref.at[k], g_ref.at[k, z, c, h], partner, pair_send.at[k], pair_recv.at[k])

    def pair_arrival(k):
        slot = g_ref.at[k, z, c, 1 - h]
        return remote(slot, slot, partner, pair_send.at[k], pair_recv.at[k])

    def ring_copy(k, q, direction, step):
        at = origin(direction, step - 1)
        slot = g_ref.at[k, at, c, half(q)]
        src = ws_ref.at[k] if step == 1 and q == 0 else slot
        sems = (k, q, direction, step - 1)
        return remote(src, slot, neighbours[direction], ring_send.at[sems], ring_recv.at[sems])

    def ring_arrival(k, q, direction, step):
        slot = g_ref.at[k, origin(direction, step), c, half(q)]
        sems = (k, q, direction, step - 1)
        return remote(slot, slot, neighbours[direction], ring_send.at[sems], ring_recv.at[sems])

    def core_index(direction, step):
        return step if direction == 0 else RIGHT_STEPS + step

    def core_copy(k, q, direction, step, own=False):
        at = origin(direction, step)
        slot = g_ref.at[k, at, c, half(q)]
        sems = (k, q, core_index(direction, step))
        return remote(ws_ref.at[k] if own else slot, slot, sibling, core_send.at[sems], core_recv.at[sems])

    def core_arrival(k, q, direction, step):
        slot = g_ref.at[k, origin(direction, step), 1 - c, half(q)]
        sems = (k, q, core_index(direction, step))
        return remote(slot, slot, sibling, core_send.at[sems], core_recv.at[sems])

    steps = (RIGHT_STEPS, LEFT_STEPS)

    def begin(k):
        for direction in (0, 1):
            ring_copy(k, 0, direction, 1).start()
        core_copy(k, 0, 0, 0, own=True).start()

    def begin_pair(k):
        pair_arrival(k).wait_recv()
        for direction in (0, 1):
            ring_copy(k, 1, direction, 1).start()
        core_copy(k, 1, 0, 0).start()

    for k in (0, 1):
        pair_copy(k).start()
    begin(0)
    local = [pltpu.make_async_copy(ws_ref.at[k], g_ref.at[k, z, c, h], local_sem.at[k]) for k in (0, 1)]
    for copy in local:
        copy.start()
    begin_pair(0)
    for k in (0, 1):
        for step in range(1, RIGHT_STEPS + 1):
            for q in (0, 1):
                for direction in (0, 1):
                    if step > steps[direction]:
                        continue
                    ring_arrival(k, q, direction, step).wait_recv()
                    if step < steps[direction]:
                        ring_copy(k, q, direction, step + 1).start()
                    core_copy(k, q, direction, step).start()
            if k == 0 and step == RIGHT_STEPS - 1:
                begin(1)
                begin_pair(1)
    for copy in local:
        copy.wait()
    for k in (0, 1):
        pair_copy(k).wait_send()
        for q in (0, 1):
            for direction in (0, 1):
                for step in range(1, steps[direction] + 1):
                    ring_copy(k, q, direction, step).wait_send()
                    core_copy(k, q, direction, step).wait_send()
                    core_arrival(k, q, direction, step).wait_recv()
            core_copy(k, q, 0, 0).wait_send()
            core_arrival(k, q, 0, 0).wait_recv()


def gathered(ws):
    return pl.pallas_call(
        gather_kernel,
        out_shape=jax.ShapeDtypeStruct((2, NZ, 2, 2, 7, 16, 256), jnp.bfloat16),
        in_specs=[pl.BlockSpec(memory_space=pltpu.VMEM)],
        out_specs=pl.BlockSpec(memory_space=pltpu.VMEM),
        scratch_shapes=[
            pltpu.SemaphoreType.DMA((2,)),
            pltpu.SemaphoreType.DMA((2,)),
            pltpu.SemaphoreType.DMA((2,)),
            pltpu.SemaphoreType.DMA((2, 2, 2, RIGHT_STEPS)),
            pltpu.SemaphoreType.DMA((2, 2, 2, RIGHT_STEPS)),
            pltpu.SemaphoreType.DMA((2, 2, NZ)),
            pltpu.SemaphoreType.DMA((2, 2, NZ)),
        ],
        compiler_params=pltpu.CompilerParams(collective_id=0, has_side_effects=True, vmem_limit_bytes=24 * MIB),
    )(ws)


def row_order():
    order = np.zeros((256, 256), np.float32)
    for tap in range(4):
        for h in range(2):
            for z in range(4):
                for c in range(2):
                    for i in range(4):
                        order[tap * 64 + h * 32 + z * 8 + c * 4 + i, z * 64 + c * 32 + h * 16 + tap * 4 + i] = 1.0
    return order


def activated(values, gain_row):
    wide_values = values.astype(jnp.float32)
    scale = lax.rsqrt(jnp.mean(wide_values * wide_values, axis=-1, keepdims=True) + 1e-06)
    return jax.nn.silu(wide_values * scale * gain_row)


def order_weights(g_ref, order_ref, w_ref):
    def ordered(group, carry):
        for zq in range(4):
            rows = g_ref[0, 4 * zq : 4 * zq + 4, :, :, group].reshape(256, 256)
            sorted_rows = jnp.dot(order_ref[...], rows, preferred_element_type=jnp.float32).astype(jnp.bfloat16)
            for tap in range(4):
                for h in range(2):
                    at = tap * 64 + h * 32
                    w_ref[4 * group + tap, h * 128 + zq * 32 : h * 128 + zq * 32 + 32, :] = sorted_rows[at : at + 32]
        return carry

    lax.fori_loop(0, 7, ordered, 0)


def conv_kernel(last, ext_ref, g_ref, order_ref, side_ref, out_ref, *rest):
    if last:
        skip_ref, w_ref, a_ref = rest
    else:
        w_ref, a_ref = rest
    order_weights(g_ref, order_ref, w_ref)
    for c in range(3):
        for d in (0, 9):
            a_ref[c, d] = jnp.zeros((4, 64, 256), jnp.bfloat16)
    place = lax.broadcasted_iota(jnp.int32, (64, 256), 0)

    def fill(d, carry):
        for r in range(4):
            plane = ext_ref[d, r]
            wide = plane.astype(jnp.float32)
            a_ref[1, d + 1, r] = plane
            a_ref[0, d + 1, r] = jnp.where(place == 0, 0.0, pltpu.roll(wide, 1, 0)).astype(jnp.bfloat16)
            a_ref[2, d + 1, r] = jnp.where(place == 63, 0.0, pltpu.roll(wide, 63, 0)).astype(jnp.bfloat16)
        return carry

    lax.fori_loop(0, 8, fill, 0)

    def chunk(m, carry):
        d = m * 2
        acc = jnp.zeros((256, 256), jnp.float32)
        for tap in range(27):
            off_depth, remainder = divmod(tap, 9)
            off_rows, off_wide = divmod(remainder, 3)
            window = a_ref[off_wide, pl.ds(d + off_depth, 2), off_rows : off_rows + 2]
            acc = acc + jnp.dot(window.reshape(256, 256), w_ref[tap], preferred_element_type=jnp.float32)
        if last:
            result = side_ref[pl.ds(d, 2)].reshape(256, 256).astype(jnp.float32) + acc
        else:
            scale = lax.rsqrt(jnp.mean(acc * acc, axis=-1, keepdims=True) + 1e-06)
            v = acc * scale * side_ref[...]
            result = v / (1.0 + jnp.exp(-v))
        out_ref[pl.ds(d, 2)] = result.astype(jnp.bfloat16).reshape(2, 2, 64, 256)
        return carry

    lax.fori_loop(0, 4, chunk, 0)
    if last:
        skip_ref[...] = w_ref[27]


def conv(last, k, ext, g, order, side):
    out_shape = [jax.ShapeDtypeStruct((8, 2, 64, 256), jnp.bfloat16)]
    if last:
        out_shape.append(jax.ShapeDtypeStruct((256, 256), jnp.bfloat16))
    whole = pl.BlockSpec(memory_space=pltpu.VMEM)
    zeros = (0,) * 6
    return pl.pallas_call(
        functools.partial(conv_kernel, last),
        grid=(1,),
        out_shape=out_shape,
        in_specs=[
            whole,
            pl.BlockSpec((1, NZ, 2, 2, 7, 16, 256), lambda i: (k,) + zeros),
            whole,
            whole,
        ],
        out_specs=[whole] * len(out_shape),
        scratch_shapes=[
            pltpu.VMEM((28, 256, 256), jnp.bfloat16),
            pltpu.VMEM((3, 10, 4, 64, 256), jnp.bfloat16),
        ],
        compiler_params=pltpu.CompilerParams(vmem_limit_bytes=48 * MIB),
    )(ext, g, order, side)


def with_halo(cells):
    head, tail = cells[:, :1], cells[:, 1:]
    count = lax.axis_size("fsdp")
    above = lax.ppermute(tail, "fsdp", [(i, i + 1) for i in range(count - 1)])
    below = lax.ppermute(head, "fsdp", [(i + 1, i) for i in range(count - 1)])
    return jnp.concatenate([above, cells, below], axis=1)


def shards(inputs, conv_first, conv_second, gain_first, gain_second, skip_weight):
    half_count = lax.axis_size("section") // 2
    decoder_pos = jnp.clip(lax.axis_index("section") - half_count, 0, half_count - 1)
    current = inputs[0]
    skip_rows = lax.dynamic_index_in_dim(skip_weight, decoder_pos, 0, keepdims=True)
    ws = jnp.stack(
        [
            jnp.concatenate([conv_first[0], jnp.zeros_like(skip_rows)], axis=0),
            jnp.concatenate([conv_second[0], skip_rows], axis=0),
        ]
    ).reshape(2, 7, 16, 256)
    g = gathered(ws)
    order = jnp.asarray(row_order(), jnp.bfloat16)
    first = activated(current, gain_first[0]).astype(jnp.bfloat16)
    (second,) = conv(False, 0, with_halo(first), g, order, gain_second)
    block, skip = conv(True, 1, with_halo(second), g, order, current)
    paired = lax.ppermute(block, "section", [(s, s + half_count) for s in range(half_count)])
    projection = jnp.dot(paired.reshape(-1, 256), skip, preferred_element_type=jnp.float32)
    return (block.astype(jnp.float32) + projection.reshape(block.shape)).astype(jnp.bfloat16)[None]


def solution(mesh):
    in_specs = (
        P("section", None, "fsdp", None, None),
        P("section", None, "fsdp", None),
        P("section", None, "fsdp", None),
        P("section", None),
        P("section", None),
        P(None, "fsdp", None),
    )
    out_specs = P("section", None, "fsdp", None, None)
    return jax.shard_map(shards, mesh=mesh, in_specs=in_specs, out_specs=out_specs, check_vma=False)
```

time: 428 us -> 136 us (0.32)
  waiting for transfers between devices: 244 us -> 17.2 us
  Pallas kernels: 0 us -> 85.4 us
  blocking collectives: 76.4 us -> 0 us
  local copies, waits for them, and re-layouts: 40.9 us -> 3.92 us
  matrix products: 20.6 us -> 1.08 us
  between operations: 13.7 us -> 0.2 us
    all_gather x3 -> x0, waiting for transfers between devices: 243 us -> none  [the longest x2 243 us: layer_kernel(): return lax.all_gather(kernel_shard, 'fsdp', axis=1, tiled=True)]
    pallas_call x0 -> x3, Pallas kernels: none -> 85.4 us  [the longest x1 66.9 us: gathered(): pl.pallas_call(gather_kernel, out_shape=jax.ShapeDtypeStruct((2, NZ, 2, 2...]
    all_gather x1 -> x0, blocking collectives: 76.4 us -> none  [shards(): full_skip = lax.all_gather(local_rows, 'fsdp', axis=0, tiled=True)]
    slice x10 -> x2, local copies, waits for them, and re-layouts: 35.4 us -> 0.08 us  [with_halo(): head, tail = (cells[:, :1], cells[:, 1:])]
    dot_general x55 -> x1, matrix products: 20.6 us -> 1.08 us  [shards(): jnp.dot(paired.reshape(-1, 256), skip, preferred_element_type=jnp.float32)]
    ppermute x4 -> x5, waiting for transfers between devices: 1.13 us -> 17.2 us  [the longest x1 13.4 us: shards(): lax.ppermute(block, 'section', [(s, s + half_count) for s in range(half_c...]
    ppermute x4 -> x5, starting transfers between devices: 22.6 us -> 23.9 us  [the longest x2 18.4 us: with_halo(): below = lax.ppermute(head, 'fsdp', [(i + 1, i) for i in range(count - 1)])]
  transfers between devices with their start and end apart: 7 -> 5, of which waited for: 3 -> 3; matrix products, arithmetic and copies ran while one was open for 11% -> 1% of each run, Pallas kernels for 0% -> 49%
where the time goes in v1:
time: 136 us
  Pallas kernels  85.4 us (63%)
  starting transfers between devices  23.9 us (18%)
  waiting for transfers between devices  17.2 us (13%)
  local copies, waits for them, and re-layouts  3.92 us (3%)
  other arithmetic  3.87 us (3%)
    pallas_call x1, Pallas kernels, gathered(): pl.pallas_call(gather_kernel, out_shape=jax.ShapeDtypeStruct((2, NZ, 2, 2...  66.9 us
    pallas_call x2, Pallas kernels, conv(): pl.pallas_call(functools.partial(conv_kernel, last), grid=(1,), out_shape...  18.5 us
    ppermute x2, starting transfers between devices, with_halo(): below = lax.ppermute(head, 'fsdp', [(i + 1, i) for i in range(count - 1)])  18.4 us
    ppermute x1, waiting for transfers between devices, shards(): lax.ppermute(block, 'section', [(s, s + half_count) for s in range(half_c...  13.4 us
    ppermute x2, starting transfers between devices, with_halo(): above = lax.ppermute(tail, 'fsdp', [(i, i + 1) for i in range(count - 1)])  4.18 us
    unnamed x10, local copies, waits for them, and re-layouts  2.94 us
  transfers between devices with their start and end apart: 5, of which 3 were waited for; matrix products, arithmetic and copies ran while one was open for 1% of the time, Pallas kernels for 49%

profile of v1, /device:TPU:24, one launch (start us, length us, event | category | flops | bytes accessed | tf_op | source)
XLA Modules:
  0.0 135.7 jit_solution(16074284123134113515)
XLA Ops:
  0.0 0.0 copy-start
  0.0 0.0 copy-start.3
  0.0 0.0 copy-start.4
  0.0 1.3 fusion
  1.3 1.4 %fusion.7 = bf16[8,2,64,256]{3,2,1,0:T(8,128)(2,1)S(1)} fusion(f32[256]{0:T(256)} %bitcast.19, f32[8,2,64]{2,1,0:T(2,128)S(1)} %add_rsqrt_fusion, bf16[1,8,2,64,256]{4,3,2,1,0:T(8,128)(2,1)} %param.7), kind=kLoop, calls=%fused_computation.9 | loop fusion | flops 2097152 | bytes 1053696 | tf_op jit(solution)/shard_map/convert_element_type | solution.py:266
  2.8 1.9 %collective-permute-start = (bf16[8,1,64,256]{3,2,1,0:T(8,128)(2,1)S(1)}, bf16[8,1,64,256]{3,2,1,0:T(8,128)(2,1)S(1)}, u32[]{:S(2)}, u32[]{:S(2)}) collective-permute-start(bf16[8,1,64,256]{3,2,1,0:T(8,128)(2,1)S(1)} %get-tuple-element.11), channel_id=1, source_target_pairs={{0,1},{1,2},{2,3},{3,4},{4,5},{5,6},{6,7},{7,8},{8,9},{9,10},{10,1... | collective-permute-start | bytes 786440 | tf_op jit(solution)/shard_map/ppermute | solution.py:248
  4.8 11.5 %collective-permute-start.1 = (bf16[8,1,64,256]{3,2,1,0:T(8,128)(2,1)S(1)}, bf16[8,1,64,256]{3,2,1,0:T(8,128)(2,1)S(1)}, u32[]{:S(2)}, u32[]{:S(2)}) collective-permute-start(bf16[8,1,64,256]{3,2,1,0:T(8,128)(2,1)S(1)} %get-tuple-element.12), channel_id=1, source_target_pairs={{1,0},{2,1},{3,2},{4,3},{5,4},{6,5},{7,6},{8,7},{9,8},{10,9},{11,1... | collective-permute-start | bytes 786440 | tf_op jit(solution)/shard_map/ppermute | solution.py:249
  16.3 0.0 copy-done
  16.3 0.9 pad_maximum_fusion.3
  17.2 0.8 concatenate.14
  18.1 66.9 %shard_map.73.g_ref = bf16[2,16,2,2,7,16,256]{6,5,4,3,2,1,0:T(8,128)(2,1)S(1)} custom-call(bf16[2,7,16,256]{3,2,1,0:T(8,128)(2,1)S(1)} %pad_maximum_fusion.2.ws_ref), custom_call_target="tpu_custom_call" | custom-call | tf_op jit(solution)/shard_map/pallas_call | solution.py:127
  85.0 0.0 copy-start.1
  85.0 2.9 %copy-done.1 = bf16[2,16,2,2,7,16,256]{6,5,4,3,2,1,0:T(8,128)(2,1)} copy-done((bf16[2,16,2,2,7,16,256]{6,5,4,3,2,1,0:T(8,128)(2,1)}, bf16[2,16,2,2,7,16,256]{6,5,4,3,2,1,0:T(8,128)(2,1)S(1)}, u32[]{:S(2)}) %copy-start.1) | copy-done | bytes 7340056
  87.9 0.0 copy-start.2
  87.9 0.0 collective-permute-done
  87.9 0.0 collective-permute-done.1
  87.9 0.1 pad_maximum_fusion.ext_ref
  88.1 0.0 copy-done.3
  88.1 0.0 copy-done.4
  88.1 9.5 %shard_map.74 = bf16[8,2,64,256]{3,2,1,0:T(8,128)(2,1)S(1)} custom-call(bf16[8,4,64,256]{3,2,1,0:T(8,128)(2,1)S(1)} %pad_maximum_fusion.ext_ref, bf16[2,16,2,2,7,16,256]{6,5,4,3,2,1,0:T(8,128)(2,1)} %copy-done.1, bf16[256,256]{1,0:T(8,128)(2,1)S(1)} %copy-done.3, f32[1,256]{1,0:T(1,128)S(1)} %copy-done.4), custom_call_target="tpu_custom_call" | custom-call | tf_op jit(solution)/shard_map/pallas_call | solution.py:226
  97.7 2.3 %collective-permute-start.2 = (bf16[8,1,64,256]{3,2,1,0:T(8,128)(2,1)S(1)}, bf16[8,1,64,256]{3,2,1,0:T(8,128)(2,1)S(1)}, u32[]{:S(2)}, u32[]{:S(2)}) collective-permute-start(bf16[8,1,64,256]{3,2,1,0:T(8,128)(2,1)S(1)} %get-tuple-element.9), channel_id=1, source_target_pairs={{0,1},{1,2},{2,3},{3,4},{4,5},{5,6},{6,7},{7,8},{8,9},{9,10},{10,1... | collective-permute-start | bytes 786440 | tf_op jit(solution)/shard_map/ppermute | solution.py:248
  99.9 6.9 %collective-permute-start.3 = (bf16[8,1,64,256]{3,2,1,0:T(8,128)(2,1)S(1)}, bf16[8,1,64,256]{3,2,1,0:T(8,128)(2,1)S(1)}, u32[]{:S(2)}, u32[]{:S(2)}) collective-permute-start(bf16[8,1,64,256]{3,2,1,0:T(8,128)(2,1)S(1)} %get-tuple-element.10), channel_id=1, source_target_pairs={{1,0},{2,1},{3,2},{4,3},{5,4},{6,5},{7,6},{8,7},{9,8},{10,9},{11,1... | collective-permute-start | bytes 786440 | tf_op jit(solution)/shard_map/ppermute | solution.py:249
  106.9 2.1 %collective-permute-done.2 = bf16[8,1,64,256]{3,2,1,0:T(8,128)(2,1)S(1)} collective-permute-done((bf16[8,1,64,256]{3,2,1,0:T(8,128)(2,1)S(1)}, bf16[8,1,64,256]{3,2,1,0:T(8,128)(2,1)S(1)}, u32[]{:S(2)}, u32[]{:S(2)}) %collective-permute-start.2) | collective-permute-done | bytes 262176 | tf_op jit(solution)/shard_map/ppermute | solution.py:248
  109.0 1.8 %collective-permute-done.3 = bf16[8,1,64,256]{3,2,1,0:T(8,128)(2,1)S(1)} collective-permute-done((bf16[8,1,64,256]{3,2,1,0:T(8,128)(2,1)S(1)}, bf16[8,1,64,256]{3,2,1,0:T(8,128)(2,1)S(1)}, u32[]{:S(2)}, u32[]{:S(2)}) %collective-permute-start.3) | collective-permute-done | bytes 262176 | tf_op jit(solution)/shard_map/ppermute | solution.py:249
  110.7 0.1 pad_maximum_fusion.1.ext_ref
  110.9 0.0 copy-done.2
  110.9 9.0 %shard_map.75 = (bf16[8,2,64,256]{3,2,1,0:T(8,128)(2,1)S(1)}, bf16[256,256]{1,0:T(8,128)(2,1)S(1)}) custom-call(bf16[8,4,64,256]{3,2,1,0:T(8,128)(2,1)S(1)} %pad_maximum_fusion.1.ext_ref, bf16[2,16,2,2,7,16,256]{6,5,4,3,2,1,0:T(8,128)(2,1)} %copy-done.1, bf16[256,256]{1,0:T(8,128)(2,1)S(1)} %copy-done.3, bf16[8,2,64,256]{3,2,1,0:T(8,128)(2,1)S(1)} %bitcast.16), custom_call_target="tpu_custom_call" | custom-call | tf_op jit(solution)/shard_map/pallas_call | solution.py:226
  119.9 1.3 collective-permute-start.4
  121.2 13.4 %collective-permute-done.4 = bf16[8,2,64,256]{3,2,1,0:T(8,128)(2,1)S(1)} collective-permute-done((bf16[8,2,64,256]{3,2,1,0:T(8,128)(2,1)S(1)}, bf16[8,2,64,256]{3,2,1,0:T(8,128)(2,1)S(1)}, u32[]{:S(2)}, u32[]{:S(2)}) %collective-permute-start.4) | collective-permute-done | bytes 524320 | tf_op jit(solution)/shard_map/ppermute | solution.py:269
  134.6 1.1 fusion.8
  (7 shorter events, 0.2 us)
Async XLA Ops:
  0.0 16.3 %copy-start = (bf16[4,4,256]{2,1,0:T(4,128)(2,1)S(1)}, bf16[4,4,256]{2,1,0:T(4,128)(2,1)}, u32[]{:S(2)}) copy-start(bf16[4,4,256]{2,1,0:T(4,128)(2,1)} %param.12) | copy-start | bytes 24580
  0.0 88.1 %copy-start.3 = (bf16[256,256]{1,0:T(8,128)(2,1)S(1)}, bf16[256,256]{1,0:T(8,128)(2,1)}, u32[]{:S(2)}) copy-start(bf16[256,256]{1,0:T(8,128)(2,1)} %constant.32.clone.order_ref) | copy-start | bytes 393220
  0.0 88.1 %copy-start.4 = (f32[1,256]{1,0:T(1,128)S(1)}, f32[1,256]{1,0:T(1,128)}, u32[]{:S(2)}) copy-start(f32[1,256]{1,0:T(1,128)} %side_ref.1) | copy-start | bytes 3076
  2.8 85.1 %collective-permute-start = (bf16[8,1,64,256]{3,2,1,0:T(8,128)(2,1)S(1)}, bf16[8,1,64,256]{3,2,1,0:T(8,128)(2,1)S(1)}, u32[]{:S(2)}, u32[]{:S(2)}) collective-permute-start(bf16[8,1,64,256]{3,2,1,0:T(8,128)(2,1)S(1)} %get-tuple-element.11), channel_id=1, source_target_pairs={{0,1},{1,2},{2,3},{3,4},{4,5},{5,6},{6,7},{7,8},{8,9},{9,10},{10,1... | collective-permute-start | bytes 786440 | tf_op jit(solution)/shard_map/ppermute | solution.py:248
  4.8 83.2 %collective-permute-start.1 = (bf16[8,1,64,256]{3,2,1,0:T(8,128)(2,1)S(1)}, bf16[8,1,64,256]{3,2,1,0:T(8,128)(2,1)S(1)}, u32[]{:S(2)}, u32[]{:S(2)}) collective-permute-start(bf16[8,1,64,256]{3,2,1,0:T(8,128)(2,1)S(1)} %get-tuple-element.12), channel_id=1, source_target_pairs={{1,0},{2,1},{3,2},{4,3},{5,4},{6,5},{7,6},{8,7},{9,8},{10,9},{11,1... | collective-permute-start | bytes 786440 | tf_op jit(solution)/shard_map/ppermute | solution.py:249
  85.0 2.9 %copy-start.1 = (bf16[2,16,2,2,7,16,256]{6,5,4,3,2,1,0:T(8,128)(2,1)}, bf16[2,16,2,2,7,16,256]{6,5,4,3,2,1,0:T(8,128)(2,1)S(1)}, u32[]{:S(2)}) copy-start(bf16[2,16,2,2,7,16,256]{6,5,4,3,2,1,0:T(8,128)(2,1)S(1)} %shard_map.73.g_ref) | copy-start | bytes 22020100
  87.9 22.9 %copy-start.2 = (bf16[1,8,2,64,256]{4,3,2,1,0:T(8,128)(2,1)S(1)}, bf16[1,8,2,64,256]{4,3,2,1,0:T(8,128)(2,1)}, u32[]{:S(2)}) copy-start(bf16[1,8,2,64,256]{4,3,2,1,0:T(8,128)(2,1)} %param.7) | copy-start | bytes 1572868
  97.7 11.3 %collective-permute-start.2 = (bf16[8,1,64,256]{3,2,1,0:T(8,128)(2,1)S(1)}, bf16[8,1,64,256]{3,2,1,0:T(8,128)(2,1)S(1)}, u32[]{:S(2)}, u32[]{:S(2)}) collective-permute-start(bf16[8,1,64,256]{3,2,1,0:T(8,128)(2,1)S(1)} %get-tuple-element.9), channel_id=1, source_target_pairs={{0,1},{1,2},{2,3},{3,4},{4,5},{5,6},{6,7},{7,8},{8,9},{9,10},{10,1... | collective-permute-start | bytes 786440 | tf_op jit(solution)/shard_map/ppermute | solution.py:248
  99.9 10.8 %collective-permute-start.3 = (bf16[8,1,64,256]{3,2,1,0:T(8,128)(2,1)S(1)}, bf16[8,1,64,256]{3,2,1,0:T(8,128)(2,1)S(1)}, u32[]{:S(2)}, u32[]{:S(2)}) collective-permute-start(bf16[8,1,64,256]{3,2,1,0:T(8,128)(2,1)S(1)} %get-tuple-element.10), channel_id=1, source_target_pairs={{1,0},{2,1},{3,2},{4,3},{5,4},{6,5},{7,6},{8,7},{9,8},{10,9},{11,1... | collective-permute-start | bytes 786440 | tf_op jit(solution)/shard_map/ppermute | solution.py:249
  119.9 14.7 %collective-permute-start.4 = (bf16[8,2,64,256]{3,2,1,0:T(8,128)(2,1)S(1)}, bf16[8,2,64,256]{3,2,1,0:T(8,128)(2,1)S(1)}, u32[]{:S(2)}, u32[]{:S(2)}) collective-permute-start(bf16[8,2,64,256]{3,2,1,0:T(8,128)(2,1)S(1)} %get-tuple-element.7), channel_id=1, source_target_pairs={{0,256},{64,320},{128,384},{192,448},{1,257},{65,321},{129,385},{1... | collective-permute-start | bytes 1572872 | tf_op jit(solution)/shard_map/ppermute | solution.py:269

commit v2 on v1

v2 whole, which is shorter than its diff:
```python
import jax
import jax.numpy as jnp
import numpy as np
from jax import lax
from jax.experimental import pallas as pl
from jax.experimental.pallas import tpu as pltpu
from jax.sharding import PartitionSpec as P

MESH = pl.DeviceIdType.MESH
NZ = 16
RIGHT_STEPS = 8
LEFT_STEPS = 7
LAG = 0
CHUNKS = 4
MIB = 1 << 20


def row_order():
    order = np.zeros((256, 256), np.float32)
    for tap in range(4):
        for h in range(2):
            for z in range(4):
                for c in range(2):
                    for i in range(4):
                        order[tap * 64 + h * 32 + z * 8 + c * 4 + i, z * 64 + c * 32 + h * 16 + tap * 4 + i] = 1.0
    return order


def normed(values, gain_row):
    scale = lax.rsqrt(jnp.mean(values * values, axis=-1, keepdims=True) + 1e-06)
    v = values * scale * gain_row
    return (v / (1.0 + jnp.exp(-v))).astype(jnp.bfloat16)


def order_weights(g_ref, k, order_ref, w_ref):
    def ordered(group, carry):
        for zq in range(4):
            rows = g_ref[k, 4 * zq : 4 * zq + 4, :, :, group].reshape(256, 256)
            sorted_rows = jnp.dot(order_ref[...], rows, preferred_element_type=jnp.float32).astype(jnp.bfloat16)
            for tap in range(4):
                for h in range(2):
                    at = tap * 64 + h * 32
                    w_ref[4 * group + tap, h * 128 + zq * 32 : h * 128 + zq * 32 + 32, :] = sorted_rows[at : at + 32]
        return carry

    lax.fori_loop(0, 7, ordered, 0)


def put_plane(a_ref, d, r, plane):
    place = lax.broadcasted_iota(jnp.int32, (64, 256), 0)
    wide = plane.astype(jnp.float32)
    a_ref[1, d + 1, r] = plane
    a_ref[0, d + 1, r] = jnp.where(place == 0, 0.0, pltpu.roll(wide, 1, 0)).astype(jnp.bfloat16)
    a_ref[2, d + 1, r] = jnp.where(place == 63, 0.0, pltpu.roll(wide, 63, 0)).astype(jnp.bfloat16)


def taps(a_ref, w_ref, d):
    acc = jnp.zeros((256, 256), jnp.float32)
    for tap in range(27):
        off_depth, remainder = divmod(tap, 9)
        off_rows, off_wide = divmod(remainder, 3)
        window = a_ref[off_wide, pl.ds(d + off_depth, 2), off_rows : off_rows + 2]
        acc = acc + jnp.dot(window.reshape(256, 256), w_ref[tap], preferred_element_type=jnp.float32)
    return acc


def level_kernel(
    x_ref, ws_ref, order_ref, gain1_ref, gain2_ref, out_ref,
    g_ref, w_ref, a1_ref, a2_ref, f_ref, halo_ref, block_ref, skip_in_ref,
    local_sem, pair_send, pair_recv, ring_send, ring_recv, core_send, core_recv, halo_send, halo_recv, skip_send, skip_recv,
):
    section = lax.axis_index("section")
    me = lax.axis_index("fsdp")
    h, z, c = me // 32, (me // 2) % NZ, me % 2

    def device(h_at, z_at, c_at):
        return (section, h_at * 32 + z_at * 2 + c_at)

    partner = device(1 - h, z, c)
    sibling = device(h, z, 1 - c)
    neighbours = (device(h, (z + 1) % NZ, c), device(h, (z + NZ - 1) % NZ, c))
    above, below = (section, (me + 63) % 64), (section, (me + 1) % 64)
    paired = ((section + 4) % 8, me)

    barrier = pltpu.get_barrier_semaphore()
    for other in (partner, sibling, above, below, paired) + neighbours:
        pl.semaphore_signal(barrier, inc=1, device_id=other, device_id_type=MESH)
    pl.semaphore_wait(barrier, 7)

    def half(q):
        return h if q == 0 else 1 - h

    def origin(direction, step):
        return (z + NZ - step) % NZ if direction == 0 else (z + step) % NZ

    def remote(src, slot, to, send, recv):
        return pltpu.make_async_remote_copy(
            src_ref=src, dst_ref=slot, send_sem=send, recv_sem=recv, device_id=to, device_id_type=MESH
        )

    def pair_copy(k):
        return remote(ws_ref.at[k], g_ref.at[k, z, c, h], partner, pair_send.at[k], pair_recv.at[k])

    def pair_arrival(k):
        slot = g_ref.at[k, z, c, 1 - h]
        return remote(slot, slot, partner, pair_send.at[k], pair_recv.at[k])

    def ring_copy(k, q, direction, step):
        at = origin(direction, step - 1)
        slot = g_ref.at[k, at, c, half(q)]
        src = ws_ref.at[k] if step == 1 and q == 0 else slot
        sems = (k, q, direction, step - 1)
        return remote(src, slot, neighbours[direction], ring_send.at[sems], ring_recv.at[sems])

    def ring_arrival(k, q, direction, step):
        slot = g_ref.at[k, origin(direction, step), c, half(q)]
        sems = (k, q, direction, step - 1)
        return remote(slot, slot, neighbours[direction], ring_send.at[sems], ring_recv.at[sems])

    def core_index(direction, step):
        return step if direction == 0 else RIGHT_STEPS + step

    def core_copy(k, q, direction, step, own=False):
        slot = g_ref.at[k, origin(direction, step), c, half(q)]
        sems = (k, q, core_index(direction, step))
        return remote(ws_ref.at[k] if own else slot, slot, sibling, core_send.at[sems], core_recv.at[sems])

    def core_arrival(k, q, direction, step):
        slot = g_ref.at[k, origin(direction, step), 1 - c, half(q)]
        sems = (k, q, core_index(direction, step))
        return remote(slot, slot, sibling, core_send.at[sems], core_recv.at[sems])

    steps = (RIGHT_STEPS, LEFT_STEPS)

    def begin(k):
        for direction in (0, 1):
            ring_copy(k, 0, direction, 1).start()
        core_copy(k, 0, 0, 0, own=True).start()

    def begin_pair(k):
        pair_arrival(k).wait_recv()
        for direction in (0, 1):
            ring_copy(k, 1, direction, 1).start()
        core_copy(k, 1, 0, 0).start()

    def core_wait(k):
        for q in (0, 1):
            core_arrival(k, q, 0, 0).wait_recv()
            for direction in (0, 1):
                for step in range(1, steps[direction] + 1):
                    core_arrival(k, q, direction, step).wait_recv()

    def halo_copy(k, row, m):
        span = pl.ds(2 * m, 2)
        return remote(
            f_ref.at[k, span, row], halo_ref.at[k, 1 - row, span], above if row == 0 else below,
            halo_send.at[k, row, m], halo_recv.at[k, 1 - row, m],
        )

    def halo_arrival(k, side, m):
        slot = halo_ref.at[k, side, pl.ds(2 * m, 2)]
        return remote(slot, slot, above if side == 0 else below, halo_send.at[k, side, m], halo_recv.at[k, side, m])

    inner = (me > 0, me < 63)

    def halo_start(k, m):
        for row in (0, 1):
            @pl.when(inner[row])
            def _():
                halo_copy(k, row, m).start()

    def halo_sent(k):
        for row in (0, 1):
            @pl.when(inner[row])
            def _():
                for m in range(CHUNKS):
                    halo_copy(k, row, m).wait_send()

    def halo_fill(k, a_ref):
        for side in (0, 1):
            @pl.when(inner[side])
            def _():
                for m in range(CHUNKS):
                    halo_arrival(k, side, m).wait_recv()

            @pl.when(jnp.logical_not(inner[side]))
            def _():
                halo_ref[k, side] = jnp.zeros((8, 64, 256), jnp.bfloat16)

        def fill(d, carry):
            for side in (0, 1):
                put_plane(a_ref, d, 3 * side, halo_ref[k, side, d])
            return carry

        lax.fori_loop(0, 8, fill, 0)

    def activate(d, carry):
        values = normed(x_ref[d].reshape(128, 256).astype(jnp.float32), gain1_ref[...])
        for r in range(2):
            plane = values[64 * r : 64 * r + 64]
            f_ref[0, d, r] = plane
            put_plane(a1_ref, d, r + 1, plane)
        return carry

    def first_chunk(m):
        values = normed(taps(a1_ref, w_ref, 2 * m), gain2_ref[...])
        for dd in range(2):
            for r in range(2):
                at = (2 * dd + r) * 64
                f_ref[1, 2 * m + dd, r] = values[at : at + 64]
                put_plane(a2_ref, 2 * m + dd, r + 1, values[at : at + 64])
        halo_start(1, m)

    for k in (0, 1):
        pair_copy(k).start()
    begin(0)
    if LAG == 0:
        begin(1)
    local = [pltpu.make_async_copy(ws_ref.at[k], g_ref.at[k, z, c, h], local_sem.at[k]) for k in (0, 1)]
    for copy in local:
        copy.start()
    lax.fori_loop(0, 8, activate, 0)
    for m in range(CHUNKS):
        halo_start(0, m)
    begin_pair(0)
    if LAG == 0:
        begin_pair(1)
    for ref in (a1_ref, a2_ref):
        for off in range(3):
            for d in (0, 9):
                ref[off, d] = jnp.zeros((4, 64, 256), jnp.bfloat16)
    for index in range(1, RIGHT_STEPS + LAG + 1):
        for q in (0, 1):
            for k in (0, 1):
                step = index - LAG * k
                for direction in (0, 1):
                    if step < 1 or step > steps[direction]:
                        continue
                    ring_arrival(k, q, direction, step).wait_recv()
                    if step < steps[direction]:
                        ring_copy(k, q, direction, step + 1).start()
                    core_copy(k, q, direction, step).start()
        if index == LAG:
            begin(1)
            begin_pair(1)
        if index == 2:
            halo_fill(0, a1_ref)
        if index == RIGHT_STEPS + min(LAG, 1):
            local[0].wait()
            core_wait(0)
            order_weights(g_ref, 0, order_ref, w_ref)
        m = index - RIGHT_STEPS - 2
        if 0 <= m < CHUNKS:
            first_chunk(m)
    for m in range(max(0, LAG - 1), CHUNKS):
        first_chunk(m)
    local[1].wait()
    core_wait(1)
    order_weights(g_ref, 1, order_ref, w_ref)
    halo_fill(1, a2_ref)

    def skip_copy(m):
        span = pl.ds(2 * m, 2)
        return remote(block_ref.at[span], skip_in_ref.at[span], paired, skip_send.at[m], skip_recv.at[m])

    def second_chunk(m, carry):
        span = pl.ds(2 * m, 2)
        values = x_ref[span].reshape(256, 256).astype(jnp.float32) + taps(a2_ref, w_ref, 2 * m)
        values = values.astype(jnp.bfloat16).reshape(2, 2, 64, 256)
        block_ref[span] = values
        out_ref[span] = values

        @pl.when(section < 4)
        def _():
            skip_copy(m).start()

        return carry

    lax.fori_loop(0, CHUNKS, second_chunk, 0)

    @pl.when(section >= 4)
    def _():
        def join(m, carry):
            skip_copy(m).wait_recv()
            span = pl.ds(2 * m, 2)
            projection = jnp.dot(
                skip_in_ref[span].reshape(256, 256), w_ref[27], preferred_element_type=jnp.float32
            )
            joined = block_ref[span].reshape(256, 256).astype(jnp.float32) + projection
            out_ref[span] = joined.astype(jnp.bfloat16).reshape(2, 2, 64, 256)
            return carry

        lax.fori_loop(0, CHUNKS, join, 0)

    @pl.when(section < 4)
    def _():
        for m in range(CHUNKS):
            skip_copy(m).wait_send()

    for k in (0, 1):
        halo_sent(k)
        pair_copy(k).wait_send()
        for q in (0, 1):
            core_copy(k, q, 0, 0).wait_send()
            for direction in (0, 1):
                for step in range(1, steps[direction] + 1):
                    ring_copy(k, q, direction, step).wait_send()
                    core_copy(k, q, direction, step).wait_send()


def level(x, ws, order, gain1, gain2):
    whole = pl.BlockSpec(memory_space=pltpu.VMEM)
    dma = pltpu.SemaphoreType.DMA
    return pl.pallas_call(
        level_kernel,
        out_shape=jax.ShapeDtypeStruct((8, 2, 64, 256), jnp.bfloat16),
        in_specs=[whole] * 5,
        out_specs=whole,
        scratch_shapes=[
            pltpu.VMEM((2, NZ, 2, 2, 7, 16, 256), jnp.bfloat16),
            pltpu.VMEM((28, 256, 256), jnp.bfloat16),
            pltpu.VMEM((3, 10, 4, 64, 256), jnp.bfloat16),
            pltpu.VMEM((3, 10, 4, 64, 256), jnp.bfloat16),
            pltpu.VMEM((2, 8, 2, 64, 256), jnp.bfloat16),
            pltpu.VMEM((2, 2, 8, 64, 256), jnp.bfloat16),
            pltpu.VMEM((8, 2, 64, 256), jnp.bfloat16),
            pltpu.VMEM((8, 2, 64, 256), jnp.bfloat16),
            dma((2,)),
            dma((2,)),
            dma((2,)),
            dma((2, 2, 2, RIGHT_STEPS)),
            dma((2, 2, 2, RIGHT_STEPS)),
            dma((2, 2, NZ)),
            dma((2, 2, NZ)),
            dma((2, 2, CHUNKS)),
            dma((2, 2, CHUNKS)),
            dma((CHUNKS,)),
            dma((CHUNKS,)),
        ],
        compiler_params=pltpu.CompilerParams(collective_id=0, has_side_effects=True, vmem_limit_bytes=48 * MIB),
    )(x, ws, order, gain1, gain2)


def shards(inputs, conv_first, conv_second, gain_first, gain_second, skip_weight):
    half_count = lax.axis_size("section") // 2
    decoder_pos = jnp.clip(lax.axis_index("section") - half_count, 0, half_count - 1)
    skip_rows = lax.dynamic_index_in_dim(skip_weight, decoder_pos, 0, keepdims=True)
    ws = jnp.stack(
        [
            jnp.concatenate([conv_first[0], jnp.zeros_like(skip_rows)], axis=0),
            jnp.concatenate([conv_second[0], skip_rows], axis=0),
        ]
    ).reshape(2, 7, 16, 256)
    order = jnp.asarray(row_order(), jnp.bfloat16)
    return level(inputs[0], ws, order, gain_first, gain_second)[None]


def solution(mesh):
    in_specs = (
        P("section", None, "fsdp", None, None),
        P("section", None, "fsdp", None),
        P("section", None, "fsdp", None),
        P("section", None),
        P("section", None),
        P(None, "fsdp", None),
    )
    out_specs = P("section", None, "fsdp", None, None)
    return jax.shard_map(shards, mesh=mesh, in_specs=in_specs, out_specs=out_specs, check_vma=False)
```

time: 136 us -> 90.7 us (0.67)
  starting transfers between devices: 23.9 us -> 0 us
  waiting for transfers between devices: 17.2 us -> 0 us
  other arithmetic: 3.87 us -> 0.87 us
    ppermute x5 -> x0, starting transfers between devices: 23.9 us -> none  [the longest x2 18.4 us: with_halo(): below = lax.ppermute(head, 'fsdp', [(i + 1, i) for i in range(count - 1)])]
    ppermute x5 -> x0, waiting for transfers between devices: 17.2 us -> none  [the longest x1 13.4 us: shards(): lax.ppermute(block, 'section', [(s, s + half_count) for s in range(half_c...]
    convert_element_type x1 -> x0, other arithmetic: 1.45 us -> none  [shards(): first = activated(current, gain_first[0]).astype(jnp.bfloat16)]
    pallas_call x3 -> x1, Pallas kernels: 85.4 us -> 86.3 us  [level(): pl.pallas_call(level_kernel, out_shape=jax.ShapeDtypeStruct((8, 2, 64, 25...]
    unnamed x10 -> x11, local copies, waits for them, and re-layouts: 2.94 us -> 2.35 us
  transfers between devices with their start and end apart: 5 -> 0, of which waited for: 3 -> 0; matrix products, arithmetic and copies ran while one was open for 1% -> 0% of each run, Pallas kernels for 49% -> 0%
where the time goes in v2:
time: 90.7 us; the launch traced here: 90.5 us
  Pallas kernels  86.3 us (95%)
  local copies, waits for them, and re-layouts  3.24 us (4%)
    pallas_call x1, Pallas kernels, level(): pl.pallas_call(level_kernel, out_shape=jax.ShapeDtypeStruct((8, 2, 64, 25...  86.3 us
    unnamed x11, local copies, waits for them, and re-layouts  2.35 us

profile of v2, /device:TPU:24, one launch (start us, length us, event | category | flops | bytes accessed | tf_op | source)
XLA Modules:
  0.0 90.5 jit_solution(12115075872000712477)
XLA Ops:
  0.0 0.0 copy-start
  0.0 0.0 copy-start.1
  0.0 0.7 copy-done
  0.7 0.9 pad_maximum_fusion.1
  1.6 0.8 concatenate.7
  2.5 0.0 copy-start.2
  2.5 0.0 copy-start.3
  2.5 0.0 copy-start.4
  2.5 0.0 copy-done.1
  2.5 0.8 copy-done.2
  3.4 0.0 copy-done.3
  3.4 0.0 copy-done.4
  3.4 86.3 %shard_map.73 = bf16[8,2,64,256]{3,2,1,0:T(8,128)(2,1)S(1)} custom-call(bf16[8,2,64,256]{3,2,1,0:T(8,128)(2,1)S(1)} %bitcast.5, bf16[2,7,16,256]{3,2,1,0:T(8,128)(2,1)S(1)} %pad_maximum_fusion.ws_ref, bf16[256,256]{1,0:T(8,128)(2,1)S(1)} %copy-done.2, f32[1,256]{1,0:T(1,128)S(1)} %copy-done.3, f32[1,256]{1,0:T(1,128)S(1)} %copy-done.4), custom_call_target="tpu_custom_call" | custom-call | tf_op jit(solution)/shard_map/pallas_call | solution.py:314
  89.7 0.8 copy.9
  (4 shorter events, 0.1 us)
Async XLA Ops:
  0.0 0.7 copy-start
  0.0 2.5 %copy-start.1 = (bf16[1,8,2,64,256]{4,3,2,1,0:T(8,128)(2,1)S(1)}, bf16[1,8,2,64,256]{4,3,2,1,0:T(8,128)(2,1)}, u32[]{:S(2)}) copy-start(bf16[1,8,2,64,256]{4,3,2,1,0:T(8,128)(2,1)} %param.7) | copy-start | bytes 1572868
  2.5 0.9 %copy-start.2 = (bf16[256,256]{1,0:T(8,128)(2,1)S(1)}, bf16[256,256]{1,0:T(8,128)(2,1)}, u32[]{:S(2)}) copy-start(bf16[256,256]{1,0:T(8,128)(2,1)} %constant.22.clone.order_ref) | copy-start | bytes 393220
  2.5 0.9 copy-start.3
  2.5 0.9 copy-start.4

commit v3 on v2

--- a/solution.py
+++ b/solution.py
@@ -8,9 +8,8 @@
 
 MESH = pl.DeviceIdType.MESH
 NZ = 16
-RIGHT_STEPS = 8
-LEFT_STEPS = 7
-LAG = 0
+STEPS = ((8, 7), (7, 8))
+CROSS = ()
 CHUNKS = 4
 MIB = 1 << 20
 
@@ -67,7 +66,7 @@
 def level_kernel(
     x_ref, ws_ref, order_ref, gain1_ref, gain2_ref, out_ref,
     g_ref, w_ref, a1_ref, a2_ref, f_ref, halo_ref, block_ref, skip_in_ref,
-    local_sem, pair_send, pair_recv, ring_send, ring_recv, core_send, core_recv, halo_send, halo_recv, skip_send, skip_recv,
+    local_sem, pair_send, pair_recv, cross_send, cross_recv, ring_send, ring_recv, core_send, core_recv, halo_send, halo_recv, skip_send, skip_recv,
 ):
     section = lax.axis_index("section")
     me = lax.axis_index("fsdp")
@@ -85,114 +84,6 @@
     barrier = pltpu.get_barrier_semaphore()
     for other in (partner, sibling, above, below, paired) + neighbours:
         pl.semaphore_signal(barrier, inc=1, device_id=other, device_id_type=MESH)
-    pl.semaphore_wait(barrier, 7)
-
-    def half(q):
-        return h if q == 0 else 1 - h
-
-    def origin(direction, step):
-        return (z + NZ - step) % NZ if direction == 0 else (z + step) % NZ
-
-    def remote(src, slot, to, send, recv):
-        return pltpu.make_async_remote_copy(
-            src_ref=src, dst_ref=slot, send_sem=send, recv_sem=recv, device_id=to, device_id_type=MESH
-        )
-
-    def pair_copy(k):
-        return remote(ws_ref.at[k], g_ref.at[k, z, c, h], partner, pair_send.at[k], pair_recv.at[k])
-
-    def pair_arrival(k):
-        slot = g_ref.at[k, z, c, 1 - h]
-        return remote(slot, slot, partner, pair_send.at[k], pair_recv.at[k])
-
-    def ring_copy(k, q, direction, step):
-        at = origin(direction, step - 1)
-        slot = g_ref.at[k, at, c, half(q)]
-        src = ws_ref.at[k] if step == 1 and q == 0 else slot
-        sems = (k, q, direction, step - 1)
-        return remote(src, slot, neighbours[direction], ring_send.at[sems], ring_recv.at[sems])
-
-    def ring_arrival(k, q, direction, step):
-        slot = g_ref.at[k, origin(direction, step), c, half(q)]
-        sems = (k, q, direction, step - 1)
-        return remote(slot, slot, neighbours[direction], ring_send.at[sems], ring_recv.at[sems])
-
-    def core_index(direction, step):
-        return step if direction == 0 else RIGHT_STEPS + step
-
-    def core_copy(k, q, direction, step, own=False):
-        slot = g_ref.at[k, origin(direction, step), c, half(q)]
-        sems = (k, q, core_index(direction, step))
-        return remote(ws_ref.at[k] if own else slot, slot, sibling, core_send.at[sems], core_recv.at[sems])
-
-    def core_arrival(k, q, direction, step):
-        slot = g_ref.at[k, origin(direction, step), 1 - c, half(q)]
-        sems = (k, q, core_index(direction, step))
-        return remote(slot, slot, sibling, core_send.at[sems], core_recv.at[sems])
-
-    steps = (RIGHT_STEPS, LEFT_STEPS)
-
-    def begin(k):
-        for direction in (0, 1):
-            ring_copy(k, 0, direction, 1).start()
-        core_copy(k, 0, 0, 0, own=True).start()
-
-    def begin_pair(k):
-        pair_arrival(k).wait_recv()
-        for direction in (0, 1):
-            ring_copy(k, 1, direction, 1).start()
-        core_copy(k, 1, 0, 0).start()
-
-    def core_wait(k):
-        for q in (0, 1):
-            core_arrival(k, q, 0, 0).wait_recv()
-            for direction in (0, 1):
-                for step in range(1, steps[direction] + 1):
-                    core_arrival(k, q, direction, step).wait_recv()
-
-    def halo_copy(k, row, m):
-        span = pl.ds(2 * m, 2)
-        return remote(
-            f_ref.at[k, span, row], halo_ref.at[k, 1 - row, span], above if row == 0 else below,
-            halo_send.at[k, row, m], halo_recv.at[k, 1 - row, m],
-        )
-
-    def halo_arrival(k, side, m):
-        slot = halo_ref.at[k, side, pl.ds(2 * m, 2)]
-        return remote(slot, slot, above if side == 0 else below, halo_send.at[k, side, m], halo_recv.at[k, side, m])
-
-    inner = (me > 0, me < 63)
-
-    def halo_start(k, m):
-        for row in (0, 1):
-            @pl.when(inner[row])
-            def _():
-                halo_copy(k, row, m).start()
-
-    def halo_sent(k):
-        for row in (0, 1):
-            @pl.when(inner[row])
-            def _():
-                for m in range(CHUNKS):
-                    halo_copy(k, row, m).wait_send()
-
-    def halo_fill(k, a_ref):
-        for side in (0, 1):
-            @pl.when(inner[side])
-            def _():
-                for m in range(CHUNKS):
-                    halo_arrival(k, side, m).wait_recv()
-
-            @pl.when(jnp.logical_not(inner[side]))
-            def _():
-                halo_ref[k, side] = jnp.zeros((8, 64, 256), jnp.bfloat16)
-
-        def fill(d, carry):
-            for side in (0, 1):
-                put_plane(a_ref, d, 3 * side, halo_ref[k, side, d])
-            return carry
-
-        lax.fori_loop(0, 8, fill, 0)
 
     def activate(d, carry):
         values = normed(x_ref[d].reshape(128, 256).astype(jnp.float32), gain1_ref[...])
@@ -201,6 +92,131 @@
             f_ref[0, d, r] = plane
             put_plane(a1_ref, d, r + 1, plane)
         return carry
+
+    lax.fori_loop(0, 8, activate, 0)
+    for ref in (a1_ref, a2_ref):
+        for off in range(3):
+            for d in (0, 9):
+                ref[off, d] = jnp.zeros((4, 64, 256), jnp.bfloat16)
+    pl.semaphore_wait(barrier, 7)
+
+    def half(q):
+        return h if q == 0 else 1 - h
+
+    def origin(direction, step):
+        return (z + NZ - step) % NZ if direction == 0 else (z + step) % NZ
+
+    def remote(src, slot, to, send, recv):
+        return pltpu.make_async_remote_copy(
+            src_ref=src, dst_ref=slot, send_sem=send, recv_sem=recv, device_id=to, device_id_type=MESH
+        )
+
+    def pair_copy(k):
+        return remote(ws_ref.at[k], g_ref.at[k, z, c, h], partner, pair_send.at[k], pair_recv.at[k])
+
+    def pair_arrival(k):
+        slot = g_ref.at[k, z, c, 1 - h]
+        return remote(slot, slot, partner, pair_send.at[k], pair_recv.at[k])
+
+    def ring_copy(k, q, direction, step):
+        at = origin(direction, step - 1)
+        slot = g_ref.at[k, at, c, half(q)]
+        src = ws_ref.at[k] if step == 1 and q == 0 else slot
+        sems = (k, q, direction, step - 1)
+        return remote(src, slot, neighbours[direction], ring_send.at[sems], ring_recv.at[sems])
+
+    def ring_arrival(k, q, direction, step):
+        slot = g_ref.at[k, origin(direction, step), c, half(q)]
+        sems = (k, q, direction, step - 1)
+        return remote(slot, slot, neighbours[direction], ring_send.at[sems], ring_recv.at[sems])
+
+    def cross_copy(k, direction, step):
+        slot = g_ref.at[k, origin(direction, step), c, h]
+        sems = (k, direction, step - 1)
+        return remote(slot, slot, partner, cross_send.at[sems], cross_recv.at[sems])
+
+    def cross_arrival(k, direction, step):
+        slot = g_ref.at[k, origin(direction, step), c, 1 - h]
+        sems = (k, direction, step - 1)
+        return remote(slot, slot, partner, cross_send.at[sems], cross_recv.at[sems])
+
+    def crosses(q, step):
+        return q == 1 and step in CROSS
+
+    def core_index(direction, step):
+        return step if direction == 0 else NZ - step
+
+    def core_copy(k, q, direction, step, own=False):
+        slot = g_ref.at[k, origin(direction, step), c, half(q)]
+        sems = (k, q, core_index(direction, step))
+        return remote(ws_ref.at[k] if own else slot, slot, sibling, core_send.at[sems], core_recv.at[sems])
+
+    def core_arrival(k, q, direction, step):
+        slot = g_ref.at[k, origin(direction, step), 1 - c, half(q)]
+        sems = (k, q, core_index(direction, step))
+        return remote(slot, slot, sibling, core_send.at[sems], core_recv.at[sems])
+
+    def begin(k):
+        for direction in (0, 1):
+            ring_copy(k, 0, direction, 1).start()
+        core_copy(k, 0, 0, 0, own=True).start()
+
+    def begin_pair(k):
+        pair_arrival(k).wait_recv()
+        for direction in (0, 1):
+            ring_copy(k, 1, direction, 1).start()
+        core_copy(k, 1, 0, 0).start()
+
+    def core_wait(k):
+        for q in (0, 1):
+            core_arrival(k, q, 0, 0).wait_recv()
+            for direction in (0, 1):
+                for step in range(1, STEPS[q][direction] + 1):
+                    core_arrival(k, q, direction, step).wait_recv()
+
+    def halo_copy(k, row, m):
+        span = pl.ds(2 * m, 2)
+        return remote(
+            f_ref.at[k, span, row], halo_ref.at[k, 1 - row, span], above if row == 0 else below,
+            halo_send.at[k, row, m], halo_recv.at[k, 1 - row, m],
+        )
+
+    def halo_arrival(k, side, m):
+        slot = halo_ref.at[k, side, pl.ds(2 * m, 2)]
+        return remote(slot, slot, above if side == 0 else below, halo_send.at[k, side, m], halo_recv.at[k, side, m])
+
+    inner = (me > 0, me < 63)
+
+    def halo_start(k, m):
+        for row in (0, 1):
+            @pl.when(inner[row])
+            def _():
+                halo_copy(k, row, m).start()
+
+    def halo_sent(k):
+        for row in (0, 1):
+            @pl.when(inner[row])
+            def _():
+                for m in range(CHUNKS):
+                    halo_copy(k, row, m).wait_send()
+
+    def halo_fill(k, a_ref):
+        for side in (0, 1):
+            @pl.when(inner[side])
+            def _():
+                for m in range(CHUNKS):
+                    halo_arrival(k, side, m).wait_recv()
+
+            @pl.when(jnp.logical_not(inner[side]))
+            def _():
+                halo_ref[k, side] = jnp.zeros((8, 64, 256), jnp.bfloat16)
+
+        def fill(d, carry):
+            for side in (0, 1):
+                put_plane(a_ref, d, 3 * side, halo_ref[k, side, d])
+            return carry
+
+        lax.fori_loop(0, 8, fill, 0)
 
     def first_chunk(m):
         values = normed(taps(a1_ref, w_ref, 2 * m), gain2_ref[...])
@@ -213,46 +229,35 @@
 
     for k in (0, 1):
         pair_copy(k).start()
-    begin(0)
-    if LAG == 0:
-        begin(1)
+        begin(k)
     local = [pltpu.make_async_copy(ws_ref.at[k], g_ref.at[k, z, c, h], local_sem.at[k]) for k in (0, 1)]
     for copy in local:
         copy.start()
-    lax.fori_loop(0, 8, activate, 0)
     for m in range(CHUNKS):
         halo_start(0, m)
-    begin_pair(0)
-    if LAG == 0:
-        begin_pair(1)
-    for ref in (a1_ref, a2_ref):
-        for off in range(3):
-            for d in (0, 9):
-                ref[off, d] = jnp.zeros((4, 64, 256), jnp.bfloat16)
-    for index in range(1, RIGHT_STEPS + LAG + 1):
+    for k in (0, 1):
+        begin_pair(k)
+    for step in range(1, NZ // 2 + 1):
         for q in (0, 1):
             for k in (0, 1):
-                step = index - LAG * k
                 for direction in (0, 1):
-                    if step < 1 or step > steps[direction]:
+                    if step > STEPS[q][direction]:
                         continue
-                    ring_arrival(k, q, direction, step).wait_recv()
-                    if step < steps[direction]:
+                    if crosses(q, step):
+                        cross_arrival(k, direction, step).wait_recv()
+                    else:
+                        ring_arrival(k, q, direction, step).wait_recv()
+                    if step < STEPS[q][direction] and not crosses(q, step + 1):
                         ring_copy(k, q, direction, step + 1).start()
+                    if q == 0 and step in CROSS:
+                        cross_copy(k, direction, step).start()
                     core_copy(k, q, direction, step).start()
-        if index == LAG:
-            begin(1)
-            begin_pair(1)
-        if index == 2:
+        if step == 2:
             halo_fill(0, a1_ref)
-        if index == RIGHT_STEPS + min(LAG, 1):
-            local[0].wait()
-            core_wait(0)
-            order_weights(g_ref, 0, order_ref, w_ref)
-        m = index - RIGHT_STEPS - 2
-        if 0 <= m < CHUNKS:
-            first_chunk(m)
-    for m in range(max(0, LAG - 1), CHUNKS):
+    local[0].wait()
+    core_wait(0)
+    order_weights(g_ref, 0, order_ref, w_ref)
+    for m in range(CHUNKS):
         first_chunk(m)
     local[1].wait()
     core_wait(1)
@@ -303,9 +308,12 @@
         for q in (0, 1):
             core_copy(k, q, 0, 0).wait_send()
             for direction in (0, 1):
-                for step in range(1, steps[direction] + 1):
-                    ring_copy(k, q, direction, step).wait_send()
+                for step in range(1, STEPS[q][direction] + 1):
                     core_copy(k, q, direction, step).wait_send()
+                    if not crosses(q, step):
+                        ring_copy(k, q, direction, step).wait_send()
+                    if crosses(q, step):
+                        cross_copy(k, direction, step).wait_send()
 
 
 def level(x, ws, order, gain1, gain2):
@@ -328,8 +336,10 @@
             dma((2,)),
             dma((2,)),
             dma((2,)),
-            dma((2, 2, 2, RIGHT_STEPS)),
-            dma((2, 2, 2, RIGHT_STEPS)),
+            dma((2, 2, 8)),
+            dma((2, 2, 8)),
+            dma((2, 2, 2, 8)),
+            dma((2, 2, 2, 8)),
             dma((2, 2, NZ)),
             dma((2, 2, NZ)),
             dma((2, 2, CHUNKS)),

time: 90.7 us -> 89.6 us (0.988); the launches traced: 90.5 us -> 88.4 us
  Pallas kernels: 86.3 us -> 84.3 us
    pallas_call x1, Pallas kernels: 86.3 us -> 84.3 us  [level(): pl.pallas_call(level_kernel, out_shape=jax.ShapeDtypeStruct((8, 2, 64, 25...]
where the time goes in v3:
time: 89.6 us; the launch traced here: 88.4 us
  Pallas kernels  84.3 us (94%)
  local copies, waits for them, and re-layouts  3.24 us (4%)
    pallas_call x1, Pallas kernels, level(): pl.pallas_call(level_kernel, out_shape=jax.ShapeDtypeStruct((8, 2, 64, 25...  84.3 us
    unnamed x11, local copies, waits for them, and re-layouts  2.35 us

profile of v3, /device:TPU:24, one launch (start us, length us, event | category | flops | bytes accessed | tf_op | source)
XLA Modules:
  0.0 88.4 jit_solution(13689866787553953332)
XLA Ops:
  0.0 0.0 copy-start
  0.0 0.0 copy-start.1
  0.0 0.7 copy-done
  0.7 0.9 pad_maximum_fusion.1
  1.6 0.8 concatenate.7
  2.5 0.0 copy-start.2
  2.5 0.0 copy-start.3
  2.5 0.0 copy-start.4
  2.5 0.0 copy-done.1
  2.5 0.8 copy-done.2
  3.4 0.0 copy-done.3
  3.4 0.0 copy-done.4
  3.4 84.3 %shard_map.73 = bf16[8,2,64,256]{3,2,1,0:T(8,128)(2,1)S(1)} custom-call(bf16[8,2,64,256]{3,2,1,0:T(8,128)(2,1)S(1)} %bitcast.5, bf16[2,7,16,256]{3,2,1,0:T(8,128)(2,1)S(1)} %pad_maximum_fusion.ws_ref, bf16[256,256]{1,0:T(8,128)(2,1)S(1)} %copy-done.2, f32[1,256]{1,0:T(1,128)S(1)} %copy-done.3, f32[1,256]{1,0:T(1,128)S(1)} %copy-done.4), custom_call_target="tpu_custom_call" | custom-call | tf_op jit(solution)/shard_map/pallas_call | solution.py:322
  87.6 0.8 copy.9
  (4 shorter events, 0.1 us)
Async XLA Ops:
  0.0 0.7 copy-start
  0.0 2.5 %copy-start.1 = (bf16[1,8,2,64,256]{4,3,2,1,0:T(8,128)(2,1)S(1)}, bf16[1,8,2,64,256]{4,3,2,1,0:T(8,128)(2,1)}, u32[]{:S(2)}) copy-start(bf16[1,8,2,64,256]{4,3,2,1,0:T(8,128)(2,1)} %param.7) | copy-start | bytes 1572868
  2.5 0.9 %copy-start.2 = (bf16[256,256]{1,0:T(8,128)(2,1)S(1)}, bf16[256,256]{1,0:T(8,128)(2,1)}, u32[]{:S(2)}) copy-start(bf16[256,256]{1,0:T(8,128)(2,1)} %constant.22.clone.order_ref) | copy-start | bytes 393220
  2.5 0.9 %copy-start.3 = (f32[1,256]{1,0:T(1,128)S(1)}, f32[1,256]{1,0:T(1,128)}, u32[]{:S(2)}) copy-start(f32[1,256]{1,0:T(1,128)} %gain1_ref.1) | copy-start | bytes 3076
  2.5 0.9 %copy-start.4 = (f32[1,256]{1,0:T(1,128)S(1)}, f32[1,256]{1,0:T(1,128)}, u32[]{:S(2)}) copy-start(f32[1,256]{1,0:T(1,128)} %gain2_ref.1) | copy-start | bytes 3076
